TPU v7x, 128 devices: a whole 4x4x4 slice. The times are simulated.
128 devices in a mesh: gx: 16 (over y, x_hi, core), gy: 8 (over z, x_lo).
Axes of the slice: x: 4 (x_hi: 2, x_lo: 2; x = x_hi * 2 + x_lo), y: 4, z: 4, core: 2. Of those that a mesh axis runs over, the one named last changes fastest.
Arguments:
- forces: float32 [3, 24, 32, 64, 128], P(None, None, 'gx', 'gy'), may hold values from -6 to 6
- levels: int32 [32, 64, 128], P('gx', 'gy'), may hold values from 0 to 15
- supports: int32 [32, 64, 128], P('gx', 'gy'), may hold values 0 or 1
Outputs:
- filtered: float32 [32, 64, 128], P('gx', 'gy')
All inputs are finite; a program needn't handle non-finite values. No bound on the sum of `supports` on one device may be relied on, other than what follows from the above.
Results may differ from a plain program's by a relative error of at most 0.0001.
Values sent between devices are 32-bit elements; how exact they have to be, the bound alone decides.
A program may use at most 128 MiB of HBM per device.

v0:
```python
import math
import jax
import jax.numpy as jnp
import numpy as np
from jax import lax
from jax.sharding import PartitionSpec as P

CASES = 24
LEVELS = 16
ITERS = 2
load_factor = 0.2


def from_behind(value, axis, steps):
    count = lax.axis_size(axis)
    leading, last = (max(0, -steps), min(count, count - steps))
    return lax.ppermute(value, axis, [(source, source + steps) for source in range(leading, last)])


def extended_2(x, sides, width):
    for axis, dim in sides:
        count, length = (lax.axis_size(axis), x.shape[dim])
        up = [(i, (i + 1) % count) for i in range(count - 1)]
        down = [(j, i) for i, j in up]
        last = lax.slice_in_dim(x, length - width, length, axis=dim)
        leading = lax.slice_in_dim(x, 0, width, axis=dim)
        before = lax.ppermute(last, axis, up)
        after = lax.ppermute(leading, axis, down)
        x = jnp.concatenate([before, x, after], axis=dim)
    return x


def element_matrix():
    poisson = 0.3
    lame_first = poisson / ((1.0 + poisson) * (1.0 - 2.0 * poisson))
    lame_shear = 1.0 / (2.0 * (1.0 + poisson))
    elastic = np.zeros((6, 6))
    elastic[:3, :3] = lame_first
    for position in range(3):
        elastic[position, position] += 2.0 * lame_shear
        elastic[position + 3, position + 3] = lame_shear
    points = [0.5 - 0.5 / math.sqrt(3.0), 0.5 + 0.5 / math.sqrt(3.0)]
    matrix = np.zeros((24, 24))
    for point_x in points:
        for point_y in points:
            for point_z in points:
                coords = (point_x, point_y, point_z)
                strain = np.zeros((6, 24))
                for corner in range(8):
                    corner_bits = (corner >> 2 & 1, corner >> 1 & 1, corner & 1)
                    shape_values = [
                        coords[axis_n] if corner_bits[axis_n] else 1.0 - coords[axis_n]
                        for axis_n in range(3)
                    ]
                    slopes = [1.0 if corner_bits[axis_n] else -1.0 for axis_n in range(3)]
                    slope_x = slopes[0] * shape_values[1] * shape_values[2]
                    slope_y = shape_values[0] * slopes[1] * shape_values[2]
                    slope_z = shape_values[0] * shape_values[1] * slopes[2]
                    offset = 3 * corner
                    strain[0, offset] = slope_x
                    strain[1, offset + 1] = slope_y
                    strain[2, offset + 2] = slope_z
                    strain[3, offset] = slope_y
                    strain[3, offset + 1] = slope_x
                    strain[4, offset + 1] = slope_z
                    strain[4, offset + 2] = slope_y
                    strain[5, offset] = slope_z
                    strain[5, offset + 2] = slope_x
                matrix = matrix + strain.T @ elastic @ strain / 8.0
    return matrix


def corner_stack(field_in, lead_in, span_x, span_y, span_z):
    pieces = []
    for corner in range(8):
        step_x, step_y, step_z = (corner >> 2 & 1, corner >> 1 & 1, corner & 1)
        pieces.append(
            field_in[
                :,
                :,
                lead_in + step_x : lead_in + step_x + span_x,
                lead_in + step_y : lead_in + step_y + span_y,
                lead_in + step_z : lead_in + step_z + span_z,
            ]
        )
    stacked = jnp.stack(pieces, 0)
    return stacked.reshape((24,) + stacked.shape[2:])


def element_forces(extended, stiff_ext, element_stiff):
    span_x, span_y, span_z = (extended.shape[2] - 2, extended.shape[3] - 2, extended.shape[4] - 2)
    outputs = []
    for first_case in range(0, extended.shape[1], 6):
        case_group = extended[:, first_case : first_case + 6]
        gathered = corner_stack(case_group, 0, span_x + 1, span_y + 1, span_z + 1)
        product = (
            jnp.einsum("ab,bcxyz->acxyz", element_stiff, gathered, precision=lax.Precision.HIGHEST)
            * stiff_ext
        )
        product = product.reshape((8, 3) + product.shape[1:])
        summed = jnp.zeros((3, case_group.shape[1], span_x, span_y, span_z), jnp.float32)
        for corner in range(8):
            step_x, step_y, step_z = (corner >> 2 & 1, corner >> 1 & 1, corner & 1)
            summed = (
                summed
                + product[corner][
                    :,
                    :,
                    1 - step_x : 1 - step_x + span_x,
                    1 - step_y : 1 - step_y + span_y,
                    1 - step_z : 1 - step_z + span_z,
                ]
            )
        outputs.append(summed)
    return jnp.concatenate(outputs, 1)


def element_energy(extended, element_stiff):
    span_x, span_y, span_z = (extended.shape[2] - 2, extended.shape[3] - 2, extended.shape[4] - 2)
    summed = jnp.zeros((span_x, span_y, span_z), jnp.float32)
    for first_case in range(0, extended.shape[1], 6):
        case_group = extended[:, first_case : first_case + 6]
        gathered = corner_stack(case_group, 1, span_x, span_y, span_z)
        product = jnp.einsum(
            "ab,bcxyz->acxyz", element_stiff, gathered, precision=lax.Precision.HIGHEST
        )
        summed = summed + jnp.sum(gathered * product, axis=(0, 1))
    return summed


def node_diagonal(stiff_ext, free_mask, element_stiff):
    span_x, span_y, span_z = free_mask.shape
    parts = []
    for component in range(3):
        summed = jnp.zeros((span_x, span_y, span_z), jnp.float32)
        for corner in range(8):
            step_x, step_y, step_z = (corner >> 2 & 1, corner >> 1 & 1, corner & 1)
            summed = (
                summed
                + stiff_ext[
                    1 - step_x : 1 - step_x + span_x,
                    1 - step_y : 1 - step_y + span_y,
                    1 - step_z : 1 - step_z + span_z,
                ]
                * element_stiff[3 * corner + component, 3 * corner + component]
            )
        parts.append(summed)
    diagonal = jnp.stack(parts, 0)[:, None]
    return 1.0 / (free_mask * diagonal + (1.0 - free_mask))


def block_gram(first_field, second_field):
    return jnp.einsum("kcxyz,kdxyz->cd", first_field, second_field, precision=lax.Precision.HIGHEST)


def combine(field_in, mixing):
    return jnp.einsum("kcxyz,cd->kdxyz", field_in, mixing, precision=lax.Precision.HIGHEST)


def cone_filter(rimmed, density):
    span_x, span_y, span_z = density.shape
    numerator = jnp.zeros((span_x, span_y, span_z), jnp.float32)
    denominator = jnp.zeros((span_x, span_y, span_z), jnp.float32)
    for shift_x in range(-2, 3):
        for shift_y in range(-2, 3):
            for shift_z in range(-2, 3):
                weight = 2.5 - math.sqrt(shift_x * shift_x + shift_y * shift_y + shift_z * shift_z)
                if weight > 0.0:
                    window = rimmed[
                        :,
                        2 + shift_x : 2 + shift_x + span_x,
                        2 + shift_y : 2 + shift_y + span_y,
                        2 + shift_z : 2 + shift_z + span_z,
                    ]
                    numerator = numerator + weight * window[0]
                    denominator = denominator + weight * window[1]
    return numerator / (density * denominator)


def local(forces, levels, supports):
    element_stiff = jnp.asarray(element_matrix(), jnp.float32)
    free_mask = (1 - supports).astype(jnp.float32)
    density = 0.3 + 0.7 * levels.astype(jnp.float32) / (LEVELS - 1)
    stiffness = density**3
    below_x = from_behind(stiffness[-1:], "gx", 1)
    widened = jnp.concatenate([below_x, stiffness], 0)
    below_y = from_behind(widened[:, -1:], "gy", 1)
    widened = jnp.concatenate([below_y, widened], 1)
    stiff_ext = jnp.pad(widened, ((0, 0), (0, 0), (1, 0)))
    inverse = node_diagonal(stiff_ext, free_mask, element_stiff)
    load_field = load_factor * free_mask * forces
    solution = jnp.zeros_like(load_field)
    residual = load_field
    direction = inverse * residual
    kept_rims = []
    alphas_kept = []
    for iteration in range(ITERS):
        extended = extended_2(free_mask * direction, (("gx", 2), ("gy", 3)), 1)
        extended = jnp.pad(extended, ((0, 0), (0, 0), (0, 0), (0, 0), (1, 1)))
        applied = (
            free_mask * element_forces(extended, stiff_ext, element_stiff)
            + (1.0 - free_mask) * direction
        )
        image_field, extended = (applied, extended)
        kept_rims.append(extended)
        curvature, along_dir = lax.psum(
            (block_gram(direction, image_field), block_gram(direction, residual)), ("gx", "gy")
        )
        factor = jnp.linalg.cholesky(curvature)
        step_alpha = jax.scipy.linalg.cho_solve((factor, True), along_dir)
        alphas_kept.append(step_alpha)
        solution = solution + combine(direction, step_alpha)
        residual = residual - combine(image_field, step_alpha)
        if iteration + 1 < ITERS:
            scaled_res = inverse * residual
            coupling = lax.psum(block_gram(image_field, scaled_res), ("gx", "gy"))
            step_beta = -jax.scipy.linalg.cho_solve((factor, True), coupling)
            direction = scaled_res + combine(direction, step_beta)
    masked_sol = free_mask * solution
    above_x = from_behind(masked_sol[:, :, :1], "gx", -1)
    sol_wide = jnp.concatenate([masked_sol, above_x], 2)
    above_y = from_behind(sol_wide[:, :, :, :1], "gy", -1)
    sol_wide = jnp.concatenate([sol_wide, above_y], 3)
    sol_ext = jnp.pad(sol_wide, ((0, 0), (0, 0), (1, 0), (1, 0), (1, 1)))
    energy = element_energy(sol_ext, element_stiff)
    sensitivity = -3.0 * density**2 * energy / CASES
    stacked = jnp.stack([density * sensitivity, jnp.ones_like(density)], 0)
    rimmed = extended_2(stacked, (("gx", 1), ("gy", 2)), 2)
    rimmed = jnp.pad(rimmed, ((0, 0), (0, 0), (0, 0), (2, 2)))
    return cone_filter(rimmed, density)


def solution(mesh):
    return jax.shard_map(
        local,
        mesh=mesh,
        in_specs=(P(None, None, "gx", "gy", None), P("gx", "gy", None), P("gx", "gy", None)),
        out_specs=P("gx", "gy", None),
        check_vma=False,
    )
```

profile of v0, /device:TPU:8, one launch (start us, length us, event | category | flops | bytes accessed | tf_op | source)
XLA Modules:
  0.0 547.2 jit_solution(6883320357306443744)
XLA Ops:
  17.1 6.0 %collective-permute-start.3 = (f32[3,24,1,8,128]{4,0,3,2,1:T(4,128)S(1)}, f32[3,24,1,8,128]{4,0,3,2,1:T(4,128)S(1)}, u32[]{:S(2)}, u32[]{:S(2)}) collective-permute-start(f32[3,24,1,8,128]{4,0,3,2,1:T(4,128)S(1)} %get-tuple-element.102), channel_id=1, source_target_pairs={{8,0},{16,8},{24,16},{32,24},{40,32},{48,40},{56,48},{64,56},{72,6... | collective-permute-start | bytes 884744 | tf_op jit(solution)/shard_map/ppermute | solution.py:28
  36.6 7.4 %collective-permute-done.5 = f32[3,24,4,1,128]{4,0,3,2,1:T(4,128)S(1)} collective-permute-done((f32[3,24,4,1,128]{4,0,3,2,1:T(4,128)S(1)}, f32[3,24,4,1,128]{4,0,3,2,1:T(4,128)S(1)}, u32[]{:S(2)}, u32[]{:S(2)}) %collective-permute-start.5) | collective-permute-done | bytes 147488 | tf_op jit(solution)/shard_map/ppermute | solution.py:28
  67.9 7.6 %reshape.547 = f32[24,6,3,9,129]{4,0,3,2,1:T(8,128)} reshape(f32[8,3,6,3,9,129]{5,1,0,4,3,2:T(4,128)} %copy.32) | data formatting | bytes 4012416 | tf_op jit(solution)/shard_map/reshape | solution.py:87
  77.8 6.4 %copy.35 = f32[8,3,6,3,9,129]{5,1,0,4,3,2:T(4,128)} copy(f32[8,3,6,3,9,129]{5,1,4,3,2,0:T(4,128)} %fusion.46) | data formatting | bytes 4012416 | tf_op jit(solution)/shard_map/stack | solution.py:86
  84.2 7.4 %reshape.550 = f32[24,6,3,9,129]{4,0,3,2,1:T(8,128)} reshape(f32[8,3,6,3,9,129]{5,1,0,4,3,2:T(4,128)} %copy.35) | data formatting | bytes 4012416 | tf_op jit(solution)/shard_map/reshape | solution.py:87
  91.7 7.8 %multiply_bitcast_fusion.7 = f32[24,6,3,9,129]{4,0,3,2,1:T(8,128)} fusion(f32[24,6,3,9,129]{4,0,3,2,1:T(8,128)} %reshape.547, f32[24,24,1,1,1]{1,0,4,3,2:T(8,128)S(1)} %copy-done.11, f32[3,9,129]{2,1,0:T(8,128)S(1)} %pad.20), kind=kOutput, calls=%fused_computation.25 | convolution fusion | flops 144948528 | bytes 4028652 | tf_op jit(solution)/shard_map/ab,bcxyz->acxyz/dot_general | solution.py:97
  108.4 7.7 %reshape.549 = f32[24,6,3,9,129]{4,0,3,2,1:T(8,128)} reshape(f32[8,3,6,3,9,129]{5,1,0,4,3,2:T(4,128)} %copy.34) | data formatting | bytes 4012416 | tf_op jit(solution)/shard_map/reshape | solution.py:87
  116.1 7.6 %multiply_bitcast_fusion.5 = f32[24,6,3,9,129]{4,0,3,2,1:T(8,128)} fusion(f32[24,6,3,9,129]{4,0,3,2,1:T(8,128)} %reshape.549, f32[24,24,1,1,1]{1,0,4,3,2:T(8,128)S(1)} %copy-done.11, f32[3,9,129]{2,1,0:T(8,128)S(1)} %pad.20), kind=kOutput, calls=%fused_computation.23 | convolution fusion | flops 144948528 | bytes 4028652 | tf_op jit(solution)/shard_map/ab,bcxyz->acxyz/dot_general | solution.py:97
  123.7 6.5 %copy.33 = f32[8,3,6,3,9,129]{5,1,0,4,3,2:T(4,128)} copy(f32[8,3,6,3,9,129]{5,1,4,3,2,0:T(4,128)} %copy-done.6) | data formatting | bytes 4012416 | tf_op jit(solution)/shard_map/stack | solution.py:86
  130.2 7.4 %reshape.548 = f32[24,6,3,9,129]{4,0,3,2,1:T(8,128)} reshape(f32[8,3,6,3,9,129]{5,1,0,4,3,2:T(4,128)} %copy.33) | data formatting | bytes 4012416 | tf_op jit(solution)/shard_map/reshape | solution.py:87
  142.9 5.7 %slice_add_fusion.28 = (f32[3,6,2,8,128]{4,0,3,2,1:T(4,128)S(1)}, f32[3,6,2,8,128]{4,0,3,2,1:T(4,128)S(1)}) fusion(f32[24,6,3,9,129]{4,0,3,2,1:T(8,128)} %multiply_bitcast_fusion.4, f32[24,6,3,9,129]{4,0,3,2,1:T(8,128)} %multiply_bitcast_fusion.5), kind=kLoop, calls=%fused_computation.312 | loop fusion | flops 516096 | bytes 2654208 | tf_op jit(solution)/shard_map/add | solution.py:105
  156.1 67.5 %all-reduce.7 = (f32[24,24]{1,0:T(8,128)S(1)}, f32[24,24]{0,1:T(8,128)S(1)}) all-reduce(f32[24,24]{1,0:T(8,128)S(1)} %convolution_bitcast_fusion.5, f32[24,24]{0,1:T(8,128)S(1)} %convolution_bitcast_fusion.6), channel_id=1, replica_groups=mesh['gx'=16,'gy'=8] {'gx','gy'}, use_global_device_ids=true, to_apply=%region_3.5 | all-reduce | flops 1152 | bytes 9216 | tf_op jit(solution)/shard_map/psum | solution.py:206
  233.4 62.4 %psum.37 = f32[24,24]{1,0:T(8,128)S(1)} all-reduce(f32[24,24]{1,0:T(8,128)S(1)} %convolution_bitcast_fusion.3), channel_id=1, replica_groups=mesh['gx'=16,'gy'=8] {'gx','gy'}, use_global_device_ids=true, to_apply=%region_4.7 | all-reduce | flops 576 | bytes 4608 | tf_op jit(solution)/shard_map/psum | solution.py:216
  300.2 6.0 %collective-permute-start.7 = (f32[3,24,1,8,128]{4,0,3,2,1:T(4,128)S(1)}, f32[3,24,1,8,128]{4,0,3,2,1:T(4,128)S(1)}, u32[]{:S(2)}, u32[]{:S(2)}) collective-permute-start(f32[3,24,1,8,128]{4,0,3,2,1:T(4,128)S(1)} %get-tuple-element.100), channel_id=1, source_target_pairs={{8,0},{16,8},{24,16},{32,24},{40,32},{48,40},{56,48},{64,56},{72,6... | collective-permute-start | bytes 884744 | tf_op jit(solution)/shard_map/ppermute | solution.py:28
  319.2 7.2 %collective-permute-done.9 = f32[3,24,4,1,128]{4,0,3,2,1:T(4,128)S(1)} collective-permute-done((f32[3,24,4,1,128]{4,0,3,2,1:T(4,128)S(1)}, f32[3,24,4,1,128]{4,0,3,2,1:T(4,128)S(1)}, u32[]{:S(2)}, u32[]{:S(2)}) %collective-permute-start.9) | collective-permute-done | bytes 147488 | tf_op jit(solution)/shard_map/ppermute | solution.py:28
  350.3 7.4 %reshape.551 = f32[24,6,3,9,129]{4,0,3,2,1:T(8,128)} reshape(f32[8,3,6,3,9,129]{5,1,0,4,3,2:T(4,128)} %copy.47) | data formatting | bytes 4012416 | tf_op jit(solution)/shard_map/reshape | solution.py:87
  366.0 6.4 %copy.50 = f32[8,3,6,3,9,129]{5,1,0,4,3,2:T(4,128)} copy(f32[8,3,6,3,9,129]{5,1,4,3,2,0:T(4,128)} %fusion.14) | data formatting | bytes 4012416 | tf_op jit(solution)/shard_map/stack | solution.py:86
  372.4 7.4 %reshape.554 = f32[24,6,3,9,129]{4,0,3,2,1:T(8,128)} reshape(f32[8,3,6,3,9,129]{5,1,0,4,3,2:T(4,128)} %copy.50) | data formatting | bytes 4012416 | tf_op jit(solution)/shard_map/reshape | solution.py:87
  385.6 6.4 %copy.49 = f32[8,3,6,3,9,129]{5,1,0,4,3,2:T(4,128)} copy(f32[8,3,6,3,9,129]{5,1,4,3,2,0:T(4,128)} %copy-done.7) | data formatting | bytes 4012416 | tf_op jit(solution)/shard_map/stack | solution.py:86
  392.0 7.4 %reshape.553 = f32[24,6,3,9,129]{4,0,3,2,1:T(8,128)} reshape(f32[8,3,6,3,9,129]{5,1,0,4,3,2:T(4,128)} %copy.49) | data formatting | bytes 4012416 | tf_op jit(solution)/shard_map/reshape | solution.py:87
  405.1 6.5 %copy.48 = f32[8,3,6,3,9,129]{5,1,0,4,3,2:T(4,128)} copy(f32[8,3,6,3,9,129]{5,1,4,3,2,0:T(4,128)} %copy-done.8) | data formatting | bytes 4012416 | tf_op jit(solution)/shard_map/stack | solution.py:86
  411.6 7.6 %reshape.552 = f32[24,6,3,9,129]{4,0,3,2,1:T(8,128)} reshape(f32[8,3,6,3,9,129]{5,1,0,4,3,2:T(4,128)} %copy.48) | data formatting | bytes 4012416 | tf_op jit(solution)/shard_map/reshape | solution.py:87
  426.6 64.6 %all-reduce.6 = (f32[24,24]{1,0:T(8,128)S(1)}, f32[24,24]{0,1:T(8,128)S(1)}) all-reduce(f32[24,24]{1,0:T(8,128)S(1)} %convolution_bitcast_fusion.1, f32[24,24]{0,1:T(8,128)S(1)} %convolution_bitcast_fusion.2), channel_id=1, replica_groups=mesh['gx'=16,'gy'=8] {'gx','gy'}, use_global_device_ids=true, to_apply=%region_6.9 | all-reduce | flops 1152 | bytes 9216 | tf_op jit(solution)/shard_map/psum | solution.py:206
  507.3 5.9 %collective-permute-done.11 = f32[3,24,3,1,128]{4,1,3,2,0:T(8,128)S(1)} collective-permute-done((f32[3,24,3,1,128]{4,1,3,2,0:T(8,128)S(1)}, f32[3,24,3,1,128]{4,1,3,2,0:T(8,128)S(1)}, u32[]{:S(2)}, u32[]{:S(2)}) %collective-permute-start.11) | collective-permute-done | bytes 110624 | tf_op jit(solution)/shard_map/ppermute | solution.py:17
  (168 shorter events, 205.7 us)
Async XLA Ops:
  0.7 7.3 %collective-permute-start = (f32[1,8,128]{2,1,0:T(8,128)S(1)}, f32[1,8,128]{2,1,0:T(8,128)S(1)}, u32[]{:S(2)}, u32[]{:S(2)}) collective-permute-start(f32[1,8,128]{2,1,0:T(8,128)S(1)} %slice.2141), channel_id=1, source_target_pairs={{0,8},{8,16},{16,24},{24,32},{32,40},{40,48},{48,56},{56,64},{64,7... | collective-permute-start | bytes 12296 | tf_op jit(solution)/shard_map/ppermute | solution.py:17
  8.0 4.7 collective-permute-start.1
  15.1 12.7 %collective-permute-start.2 = (f32[3,24,1,8,128]{4,0,3,2,1:T(4,128)S(1)}, f32[3,24,1,8,128]{4,0,3,2,1:T(4,128)S(1)}, u32[]{:S(2)}, u32[]{:S(2)}) collective-permute-start(f32[3,24,1,8,128]{4,0,3,2,1:T(4,128)S(1)} %get-tuple-element.101), channel_id=1, source_target_pairs={{0,8},{8,16},{16,24},{24,32},{32,40},{40,48},{48,56},{56,64},{64,7... | collective-permute-start | bytes 884744 | tf_op jit(solution)/shard_map/ppermute | solution.py:27
  17.1 11.3 %collective-permute-start.3 = (f32[3,24,1,8,128]{4,0,3,2,1:T(4,128)S(1)}, f32[3,24,1,8,128]{4,0,3,2,1:T(4,128)S(1)}, u32[]{:S(2)}, u32[]{:S(2)}) collective-permute-start(f32[3,24,1,8,128]{4,0,3,2,1:T(4,128)S(1)} %get-tuple-element.102), channel_id=1, source_target_pairs={{8,0},{16,8},{24,16},{32,24},{40,32},{48,40},{56,48},{64,56},{72,6... | collective-permute-start | bytes 884744 | tf_op jit(solution)/shard_map/ppermute | solution.py:28
  28.5 8.1 %collective-permute-start.4 = (f32[3,24,4,1,128]{4,0,3,2,1:T(4,128)S(1)}, f32[3,24,4,1,128]{4,0,3,2,1:T(4,128)S(1)}, u32[]{:S(2)}, u32[]{:S(2)}) collective-permute-start(f32[3,24,4,1,128]{4,0,3,2,1:T(4,128)S(1)} %get-tuple-element.79), channel_id=1, source_target_pairs={{0,1},{1,2},{2,3},{3,4},{4,5},{5,6},{6,7},{8,9},{9,10},{10,11},{11... | collective-permute-start | bytes 442376 | tf_op jit(solution)/shard_map/ppermute | solution.py:27
  32.7 11.3 %collective-permute-start.5 = (f32[3,24,4,1,128]{4,0,3,2,1:T(4,128)S(1)}, f32[3,24,4,1,128]{4,0,3,2,1:T(4,128)S(1)}, u32[]{:S(2)}, u32[]{:S(2)}) collective-permute-start(f32[3,24,4,1,128]{4,0,3,2,1:T(4,128)S(1)} %get-tuple-element.80), channel_id=1, source_target_pairs={{1,0},{2,1},{3,2},{4,3},{5,4},{6,5},{7,6},{9,8},{10,9},{11,10},{12... | collective-permute-start | bytes 442376 | tf_op jit(solution)/shard_map/ppermute | solution.py:28
  48.2 7.3 %copy-start.1 = (f32[3,24,4,10,130]{4,0,3,2,1:T(4,128)}, f32[3,24,4,10,130]{4,0,3,2,1:T(4,128)S(1)}, u32[]{:S(2)}) copy-start(f32[3,24,4,10,130]{4,0,3,2,1:T(4,128)S(1)} %select_maximum_fusion.4) | copy-start | bytes 4492804
  84.2 7.4 %copy-start.11 = (f32[24,24,1,1,1]{1,0,4,3,2:T(8,128)S(1)}, f32[24,24,1,1,1]{1,0,4,3,2:T(8,128)}, u32[]{:S(2)}) copy-start(f32[24,24,1,1,1]{1,0,4,3,2:T(8,128)} %constant.139) | copy-start | bytes 6916
  91.6 7.8 %copy-start.2 = (f32[24,6,3,9,129]{4,0,3,2,1:T(8,128)S(1)}, f32[24,6,3,9,129]{4,0,3,2,1:T(8,128)}, u32[]{:S(2)}) copy-start(f32[24,6,3,9,129]{4,0,3,2,1:T(8,128)} %reshape.550) | copy-start | bytes 6018628
  91.6 12.8 %slice-start = ((s8[5308416]{0:T(1024)(128)(4,1)}), s8[4194304]{0:T(1024)(128)(4,1)S(1)}, s32[]{:S(2)}) async-start(s8[5308416]{0:T(1024)(128)(4,1)} %bitcast.1302), calls=%async_computation | async-start | bytes 8388608
  142.9 9.7 %copy-start.9 = (f32[3,24,2,8,128]{4,3,2,1,0:T(8,128)S(1)}, f32[3,24,2,8,128]{4,3,2,1,0:T(8,128)}, u32[]{:S(2)}) copy-start(f32[3,24,2,8,128]{4,3,2,1,0:T(8,128)} %param.7) | copy-start | bytes 1769476
  297.1 19.0 %copy-start.10 = (f32[3,24,2,8,128]{4,0,3,2,1:T(4,128)S(1)}, f32[3,24,2,8,128]{4,0,3,2,1:T(4,128)}, u32[]{:S(2)}) copy-start(f32[3,24,2,8,128]{4,0,3,2,1:T(4,128)} %get-tuple-element.14) | copy-start | bytes 1769476
  297.9 11.9 %collective-permute-start.6 = (f32[3,24,1,8,128]{4,0,3,2,1:T(4,128)S(1)}, f32[3,24,1,8,128]{4,0,3,2,1:T(4,128)S(1)}, u32[]{:S(2)}, u32[]{:S(2)}) collective-permute-start(f32[3,24,1,8,128]{4,0,3,2,1:T(4,128)S(1)} %get-tuple-element.99), channel_id=1, source_target_pairs={{0,8},{8,16},{16,24},{24,32},{32,40},{40,48},{48,56},{56,64},{64,7... | collective-permute-start | bytes 884744 | tf_op jit(solution)/shard_map/ppermute | solution.py:27
  300.2 11.3 %collective-permute-start.7 = (f32[3,24,1,8,128]{4,0,3,2,1:T(4,128)S(1)}, f32[3,24,1,8,128]{4,0,3,2,1:T(4,128)S(1)}, u32[]{:S(2)}, u32[]{:S(2)}) collective-permute-start(f32[3,24,1,8,128]{4,0,3,2,1:T(4,128)S(1)} %get-tuple-element.100), channel_id=1, source_target_pairs={{8,0},{16,8},{24,16},{32,24},{40,32},{48,40},{56,48},{64,56},{72,6... | collective-permute-start | bytes 884744 | tf_op jit(solution)/shard_map/ppermute | solution.py:28
  311.7 7.5 %collective-permute-start.8 = (f32[3,24,4,1,128]{4,0,3,2,1:T(4,128)S(1)}, f32[3,24,4,1,128]{4,0,3,2,1:T(4,128)S(1)}, u32[]{:S(2)}, u32[]{:S(2)}) collective-permute-start(f32[3,24,4,1,128]{4,0,3,2,1:T(4,128)S(1)} %get-tuple-element.77), channel_id=1, source_target_pairs={{0,1},{1,2},{2,3},{3,4},{4,5},{5,6},{6,7},{8,9},{9,10},{10,11},{11... | collective-permute-start | bytes 442376 | tf_op jit(solution)/shard_map/ppermute | solution.py:27
  314.8 11.6 %collective-permute-start.9 = (f32[3,24,4,1,128]{4,0,3,2,1:T(4,128)S(1)}, f32[3,24,4,1,128]{4,0,3,2,1:T(4,128)S(1)}, u32[]{:S(2)}, u32[]{:S(2)}) collective-permute-start(f32[3,24,4,1,128]{4,0,3,2,1:T(4,128)S(1)} %get-tuple-element.78), channel_id=1, source_target_pairs={{1,0},{2,1},{3,2},{4,3},{5,4},{6,5},{7,6},{9,8},{10,9},{11,10},{12... | collective-permute-start | bytes 442376 | tf_op jit(solution)/shard_map/ppermute | solution.py:28
  330.6 7.3 %copy-start = (f32[3,24,4,10,130]{4,0,3,2,1:T(4,128)}, f32[3,24,4,10,130]{4,0,3,2,1:T(4,128)S(1)}, u32[]{:S(2)}) copy-start(f32[3,24,4,10,130]{4,0,3,2,1:T(4,128)S(1)} %select_maximum_fusion) | copy-start | bytes 4492804
  498.1 7.6 %collective-permute-start.10 = (f32[3,24,1,8,128]{4,1,3,2,0:T(8,128)S(1)}, f32[3,24,1,8,128]{4,1,3,2,0:T(8,128)S(1)}, u32[]{:S(2)}, u32[]{:S(2)}) collective-permute-start(f32[3,24,1,8,128]{4,1,3,2,0:T(8,128)S(1)} %slice.2277), channel_id=1, source_target_pairs={{8,0},{16,8},{24,16},{32,24},{40,32},{48,40},{56,48},{64,56},{72,6... | collective-permute-start | bytes 884744 | tf_op jit(solution)/shard_map/ppermute | solution.py:17
  505.8 7.5 %collective-permute-start.11 = (f32[3,24,3,1,128]{4,1,3,2,0:T(8,128)S(1)}, f32[3,24,3,1,128]{4,1,3,2,0:T(8,128)S(1)}, u32[]{:S(2)}, u32[]{:S(2)}) collective-permute-start(f32[3,24,3,1,128]{4,1,3,2,0:T(8,128)S(1)} %pad_maximum_fusion.8), channel_id=1, source_target_pairs={{1,0},{2,1},{3,2},{4,3},{5,4},{6,5},{7,6},{9,8},{10,9},{11,10},{12... | collective-permute-start | bytes 331784 | tf_op jit(solution)/shard_map/ppermute | solution.py:17
  519.2 5.1 copy-start.12
  524.4 6.2 %collective-permute-start.13 = (f32[2,2,8,128]{3,2,1,0:T(8,128)S(1)}, f32[2,2,8,128]{3,2,1,0:T(8,128)S(1)}, u32[]{:S(2)}, u32[]{:S(2)}) collective-permute-start(f32[2,2,8,128]{3,2,1,0:T(8,128)S(1)} %stack.455), channel_id=1, source_target_pairs={{8,0},{16,8},{24,16},{32,24},{40,32},{48,40},{56,48},{64,56},{72,6... | collective-permute-start | bytes 49160 | tf_op jit(solution)/shard_map/ppermute | solution.py:28
  528.7 7.5 %collective-permute-start.12 = (f32[2,2,8,128]{3,2,1,0:T(8,128)S(1)}, f32[2,2,8,128]{3,2,1,0:T(8,128)S(1)}, u32[]{:S(2)}, u32[]{:S(2)}) collective-permute-start(f32[2,2,8,128]{3,2,1,0:T(8,128)S(1)} %stack.455), channel_id=1, source_target_pairs={{0,8},{8,16},{16,24},{24,32},{32,40},{40,48},{48,56},{56,64},{64,7... | collective-permute-start | bytes 49160 | tf_op jit(solution)/shard_map/ppermute | solution.py:27
  536.1 5.3 collective-permute-start.14
  540.1 5.6 %collective-permute-start.15 = (f32[2,6,2,128]{3,2,1,0:T(2,128)S(1)}, f32[2,6,2,128]{3,2,1,0:T(2,128)S(1)}, u32[]{:S(2)}, u32[]{:S(2)}) collective-permute-start(f32[2,6,2,128]{3,2,1,0:T(2,128)S(1)} %get-tuple-element.113), channel_id=1, source_target_pairs={{1,0},{2,1},{3,2},{4,3},{5,4},{6,5},{7,6},{9,8},{10,9},{11,10},{12... | collective-permute-start | bytes 36872 | tf_op jit(solution)/shard_map/ppermute | solution.py:28
  (7 other events, 19.1 us)
where the time goes:
time: 558 us; the launch traced here: 547 us
  blocking collectives  195 us (35%)
  local copies, waits for them, and re-layouts  142 us (25%)
  matrix products  67.7 us (12%)
  waiting for transfers between devices  54.4 us (10%)
  starting transfers between devices  47.9 us (9%)
  other arithmetic  39.2 us (7%)
    psum x2, blocking collectives, local(): lax.psum((block_gram(direction, image_field), block_gram(direction, resid...  132 us
    psum x1, blocking collectives, local(): coupling = lax.psum(block_gram(image_field, scaled_res), ('gx', 'gy'))  62.4 us
    reshape x8, local copies, waits for them, and re-layouts, corner_stack(): return stacked.reshape((24,) + stacked.shape[2:])  59.9 us
    another operation x16, local copies, waits for them, and re-layouts, corner_stack(): stacked = jnp.stack(pieces, 0)  52.4 us
    dot_general x8, matrix products, element_forces(): jnp.einsum('ab,bcxyz->acxyz', element_stiff, gathered, precision=lax.Prec...  46.9 us
    unnamed x55, local copies, waits for them, and re-layouts  29.4 us
    ppermute x6, waiting for transfers between devices, extended_2(): after = lax.ppermute(leading, axis, down)  21.1 us
    ppermute x6, starting transfers between devices, extended_2(): after = lax.ppermute(leading, axis, down)  20.2 us
  transfers between devices with their start and end apart: 16, of which 15 were waited for; matrix products, arithmetic and copies ran while one was open for 1% of the time, Pallas kernels for 0%

commit v1 on v0

--- a/solution.py
+++ b/solution.py
@@ -204,7 +204,8 @@
         image_field, extended = (applied, extended)
         kept_rims.append(extended)
         curvature, along_dir = lax.psum(
-            (block_gram(direction, image_field), block_gram(direction, residual)), ("gx", "gy")
+            lax.psum((block_gram(direction, image_field), block_gram(direction, residual)), "gx"),
+            "gy",
         )
         factor = jnp.linalg.cholesky(curvature)
         step_alpha = jax.scipy.linalg.cho_solve((factor, True), along_dir)

time: 558 us -> 612 us (1.097)
  the two profiles are of different devices: /device:TPU:8 before, /device:TPU:6 now
where the time goes in v1:
time: 612 us; the launch traced here: 601 us
  blocking collectives  252 us (41%)
  local copies, waits for them, and re-layouts  142 us (23%)
  matrix products  67.7 us (11%)
  starting transfers between devices  53.6 us (9%)
  waiting for transfers between devices  45.7 us (7%)
  other arithmetic  39.3 us (6%)
    psum x2, blocking collectives, local(): lax.psum((block_gram(direction, image_field), block_gram(direction, resid...  125 us
    psum x1, blocking collectives, local(): coupling = lax.psum(block_gram(image_field, scaled_res), ('gx', 'gy'))  68.2 us
    reshape x8, local copies, waits for them, and re-layouts, corner_stack(): return stacked.reshape((24,) + stacked.shape[2:])  59.9 us
    psum x2, blocking collectives, local(): lax.psum(lax.psum((block_gram(direction, image_field), block_gram(directi...  58.4 us
    another operation x16, local copies, waits for them, and re-layouts, corner_stack(): stacked = jnp.stack(pieces, 0)  52.3 us
    dot_general x8, matrix products, element_forces(): jnp.einsum('ab,bcxyz->acxyz', element_stiff, gathered, precision=lax.Prec...  46.9 us
    unnamed x55, local copies, waits for them, and re-layouts  29.4 us
    ppermute x6, starting transfers between devices, extended_2(): after = lax.ppermute(leading, axis, down)  25.1 us
  transfers between devices with their start and end apart: 16, of which 14 were waited for; matrix products, arithmetic and copies ran while one was open for 1% of the time, Pallas kernels for 0%

profile of v1, /device:TPU:6, one launch (start us, length us, event | category | flops | bytes accessed | tf_op | source)
XLA Modules:
  0.0 601.3 jit_solution(8449605623767116086)
XLA Ops:
  37.2 6.4 %collective-permute-done.5 = f32[3,24,4,1,128]{4,0,3,2,1:T(4,128)S(1)} collective-permute-done((f32[3,24,4,1,128]{4,0,3,2,1:T(4,128)S(1)}, f32[3,24,4,1,128]{4,0,3,2,1:T(4,128)S(1)}, u32[]{:S(2)}, u32[]{:S(2)}) %collective-permute-start.5) | collective-permute-done | bytes 147488 | tf_op jit(solution)/shard_map/ppermute | solution.py:28
  67.5 7.6 %reshape.547 = f32[24,6,3,9,129]{4,0,3,2,1:T(8,128)} reshape(f32[8,3,6,3,9,129]{5,1,0,4,3,2:T(4,128)} %copy.32) | data formatting | bytes 4012416 | tf_op jit(solution)/shard_map/reshape | solution.py:87
  77.5 6.4 %copy.35 = f32[8,3,6,3,9,129]{5,1,0,4,3,2:T(4,128)} copy(f32[8,3,6,3,9,129]{5,1,4,3,2,0:T(4,128)} %fusion.46) | data formatting | bytes 4012416 | tf_op jit(solution)/shard_map/stack | solution.py:86
  83.9 7.4 %reshape.550 = f32[24,6,3,9,129]{4,0,3,2,1:T(8,128)} reshape(f32[8,3,6,3,9,129]{5,1,0,4,3,2:T(4,128)} %copy.35) | data formatting | bytes 4012416 | tf_op jit(solution)/shard_map/reshape | solution.py:87
  91.3 7.8 %multiply_bitcast_fusion.7 = f32[24,6,3,9,129]{4,0,3,2,1:T(8,128)} fusion(f32[24,6,3,9,129]{4,0,3,2,1:T(8,128)} %reshape.547, f32[24,24,1,1,1]{1,0,4,3,2:T(8,128)S(1)} %copy-done.11, f32[3,9,129]{2,1,0:T(8,128)S(1)} %pad.20), kind=kOutput, calls=%fused_computation.25 | convolution fusion | flops 144948528 | bytes 4028652 | tf_op jit(solution)/shard_map/ab,bcxyz->acxyz/dot_general | solution.py:97
  108.0 7.8 %reshape.549 = f32[24,6,3,9,129]{4,0,3,2,1:T(8,128)} reshape(f32[8,3,6,3,9,129]{5,1,0,4,3,2:T(4,128)} %copy.34) | data formatting | bytes 4012416 | tf_op jit(solution)/shard_map/reshape | solution.py:87
  115.8 7.6 %multiply_bitcast_fusion.5 = f32[24,6,3,9,129]{4,0,3,2,1:T(8,128)} fusion(f32[24,6,3,9,129]{4,0,3,2,1:T(8,128)} %reshape.549, f32[24,24,1,1,1]{1,0,4,3,2:T(8,128)S(1)} %copy-done.11, f32[3,9,129]{2,1,0:T(8,128)S(1)} %pad.20), kind=kOutput, calls=%fused_computation.23 | convolution fusion | flops 144948528 | bytes 4028652 | tf_op jit(solution)/shard_map/ab,bcxyz->acxyz/dot_general | solution.py:97
  123.4 6.5 %copy.33 = f32[8,3,6,3,9,129]{5,1,0,4,3,2:T(4,128)} copy(f32[8,3,6,3,9,129]{5,1,4,3,2,0:T(4,128)} %copy-done.6) | data formatting | bytes 4012416 | tf_op jit(solution)/shard_map/stack | solution.py:86
  129.9 7.4 %reshape.548 = f32[24,6,3,9,129]{4,0,3,2,1:T(8,128)} reshape(f32[8,3,6,3,9,129]{5,1,0,4,3,2:T(4,128)} %copy.33) | data formatting | bytes 4012416 | tf_op jit(solution)/shard_map/reshape | solution.py:87
  142.6 5.8 slice_add_fusion.28
  155.8 63.0 %all-reduce.7 = (f32[24,24]{1,0:T(8,128)S(1)}, f32[24,24]{0,1:T(8,128)S(1)}) all-reduce(f32[24,24]{1,0:T(8,128)S(1)} %convolution_bitcast_fusion.5, f32[24,24]{0,1:T(8,128)S(1)} %convolution_bitcast_fusion.6), channel_id=1, replica_groups=mesh['gx'=16,'gy'=8] {'gx'}, use_global_device_ids=true, to_apply=%region_4.6 | all-reduce | flops 1152 | bytes 9216 | tf_op jit(solution)/shard_map/psum | solution.py:207
  218.8 29.2 %all-reduce.9 = (f32[24,24]{1,0:T(8,128)S(1)}, f32[24,24]{0,1:T(8,128)S(1)}) all-reduce(f32[24,24]{1,0:T(8,128)S(1)} %get-tuple-element.9, f32[24,24]{0,1:T(8,128)S(1)} %get-tuple-element.10), channel_id=1, replica_groups=mesh['gx'=16,'gy'=8] {'gy'}, use_global_device_ids=true, to_apply=%region_5.7 | all-reduce | flops 1152 | bytes 9216 | tf_op jit(solution)/shard_map/psum | solution.py:206
  257.8 68.2 %psum.67 = f32[24,24]{1,0:T(8,128)S(1)} all-reduce(f32[24,24]{1,0:T(8,128)S(1)} %convolution_bitcast_fusion.3), channel_id=1, replica_groups=mesh['gx'=16,'gy'=8] {'gx','gy'}, use_global_device_ids=true, to_apply=%region_6.9 | all-reduce | flops 576 | bytes 4608 | tf_op jit(solution)/shard_map/psum | solution.py:217
  349.4 5.8 collective-permute-done.9
  379.1 7.4 %reshape.551 = f32[24,6,3,9,129]{4,0,3,2,1:T(8,128)} reshape(f32[8,3,6,3,9,129]{5,1,0,4,3,2:T(4,128)} %copy.47) | data formatting | bytes 4012416 | tf_op jit(solution)/shard_map/reshape | solution.py:87
  394.8 6.4 %copy.50 = f32[8,3,6,3,9,129]{5,1,0,4,3,2:T(4,128)} copy(f32[8,3,6,3,9,129]{5,1,4,3,2,0:T(4,128)} %fusion.14) | data formatting | bytes 4012416 | tf_op jit(solution)/shard_map/stack | solution.py:86
  401.2 7.4 %reshape.554 = f32[24,6,3,9,129]{4,0,3,2,1:T(8,128)} reshape(f32[8,3,6,3,9,129]{5,1,0,4,3,2:T(4,128)} %copy.50) | data formatting | bytes 4012416 | tf_op jit(solution)/shard_map/reshape | solution.py:87
  414.4 6.4 %copy.49 = f32[8,3,6,3,9,129]{5,1,0,4,3,2:T(4,128)} copy(f32[8,3,6,3,9,129]{5,1,4,3,2,0:T(4,128)} %copy-done.7) | data formatting | bytes 4012416 | tf_op jit(solution)/shard_map/stack | solution.py:86
  420.8 7.4 %reshape.553 = f32[24,6,3,9,129]{4,0,3,2,1:T(8,128)} reshape(f32[8,3,6,3,9,129]{5,1,0,4,3,2:T(4,128)} %copy.49) | data formatting | bytes 4012416 | tf_op jit(solution)/shard_map/reshape | solution.py:87
  433.9 6.5 %copy.48 = f32[8,3,6,3,9,129]{5,1,0,4,3,2:T(4,128)} copy(f32[8,3,6,3,9,129]{5,1,4,3,2,0:T(4,128)} %copy-done.8) | data formatting | bytes 4012416 | tf_op jit(solution)/shard_map/stack | solution.py:86
  440.4 7.6 %reshape.552 = f32[24,6,3,9,129]{4,0,3,2,1:T(8,128)} reshape(f32[8,3,6,3,9,129]{5,1,0,4,3,2:T(4,128)} %copy.48) | data formatting | bytes 4012416 | tf_op jit(solution)/shard_map/reshape | solution.py:87
  455.5 62.0 %all-reduce.6 = (f32[24,24]{1,0:T(8,128)S(1)}, f32[24,24]{0,1:T(8,128)S(1)}) all-reduce(f32[24,24]{1,0:T(8,128)S(1)} %convolution_bitcast_fusion.1, f32[24,24]{0,1:T(8,128)S(1)} %convolution_bitcast_fusion.2), channel_id=1, replica_groups=mesh['gx'=16,'gy'=8] {'gx'}, use_global_device_ids=true, to_apply=%region_9.12 | all-reduce | flops 1152 | bytes 9216 | tf_op jit(solution)/shard_map/psum | solution.py:207
  517.4 29.2 %all-reduce.8 = (f32[24,24]{1,0:T(8,128)S(1)}, f32[24,24]{0,1:T(8,128)S(1)}) all-reduce(f32[24,24]{1,0:T(8,128)S(1)} %get-tuple-element.6, f32[24,24]{0,1:T(8,128)S(1)} %get-tuple-element.8), channel_id=1, replica_groups=mesh['gx'=16,'gy'=8] {'gy'}, use_global_device_ids=true, to_apply=%region_10.13 | all-reduce | flops 1152 | bytes 9216 | tf_op jit(solution)/shard_map/psum | solution.py:206
  578.5 5.9 collective-permute-start.13
  (170 shorter events, 217.0 us)
Async XLA Ops:
  0.7 6.4 %collective-permute-start = (f32[1,8,128]{2,1,0:T(8,128)S(1)}, f32[1,8,128]{2,1,0:T(8,128)S(1)}, u32[]{:S(2)}, u32[]{:S(2)}) collective-permute-start(f32[1,8,128]{2,1,0:T(8,128)S(1)} %slice.2141), channel_id=1, source_target_pairs={{0,8},{8,16},{16,24},{24,32},{32,40},{40,48},{48,56},{56,64},{64,7... | collective-permute-start | bytes 12296 | tf_op jit(solution)/shard_map/ppermute | solution.py:17
  7.1 5.5 collective-permute-start.1
  15.0 10.6 %collective-permute-start.2 = (f32[3,24,1,8,128]{4,0,3,2,1:T(4,128)S(1)}, f32[3,24,1,8,128]{4,0,3,2,1:T(4,128)S(1)}, u32[]{:S(2)}, u32[]{:S(2)}) collective-permute-start(f32[3,24,1,8,128]{4,0,3,2,1:T(4,128)S(1)} %get-tuple-element.105), channel_id=1, source_target_pairs={{0,8},{8,16},{16,24},{24,32},{32,40},{40,48},{48,56},{56,64},{64,7... | collective-permute-start | bytes 884744 | tf_op jit(solution)/shard_map/ppermute | solution.py:27
  17.0 12.2 %collective-permute-start.3 = (f32[3,24,1,8,128]{4,0,3,2,1:T(4,128)S(1)}, f32[3,24,1,8,128]{4,0,3,2,1:T(4,128)S(1)}, u32[]{:S(2)}, u32[]{:S(2)}) collective-permute-start(f32[3,24,1,8,128]{4,0,3,2,1:T(4,128)S(1)} %get-tuple-element.106), channel_id=1, source_target_pairs={{8,0},{16,8},{24,16},{32,24},{40,32},{48,40},{56,48},{64,56},{72,6... | collective-permute-start | bytes 884744 | tf_op jit(solution)/shard_map/ppermute | solution.py:28
  29.3 7.9 %collective-permute-start.4 = (f32[3,24,4,1,128]{4,0,3,2,1:T(4,128)S(1)}, f32[3,24,4,1,128]{4,0,3,2,1:T(4,128)S(1)}, u32[]{:S(2)}, u32[]{:S(2)}) collective-permute-start(f32[3,24,4,1,128]{4,0,3,2,1:T(4,128)S(1)} %get-tuple-element.83), channel_id=1, source_target_pairs={{0,1},{1,2},{2,3},{3,4},{4,5},{5,6},{6,7},{8,9},{9,10},{10,11},{11... | collective-permute-start | bytes 442376 | tf_op jit(solution)/shard_map/ppermute | solution.py:27
  33.4 10.2 %collective-permute-start.5 = (f32[3,24,4,1,128]{4,0,3,2,1:T(4,128)S(1)}, f32[3,24,4,1,128]{4,0,3,2,1:T(4,128)S(1)}, u32[]{:S(2)}, u32[]{:S(2)}) collective-permute-start(f32[3,24,4,1,128]{4,0,3,2,1:T(4,128)S(1)} %get-tuple-element.84), channel_id=1, source_target_pairs={{1,0},{2,1},{3,2},{4,3},{5,4},{6,5},{7,6},{9,8},{10,9},{11,10},{12... | collective-permute-start | bytes 442376 | tf_op jit(solution)/shard_map/ppermute | solution.py:28
  47.8 7.3 %copy-start.1 = (f32[3,24,4,10,130]{4,0,3,2,1:T(4,128)}, f32[3,24,4,10,130]{4,0,3,2,1:T(4,128)S(1)}, u32[]{:S(2)}) copy-start(f32[3,24,4,10,130]{4,0,3,2,1:T(4,128)S(1)} %select_maximum_fusion.4) | copy-start | bytes 4492804
  83.9 7.4 %copy-start.11 = (f32[24,24,1,1,1]{1,0,4,3,2:T(8,128)S(1)}, f32[24,24,1,1,1]{1,0,4,3,2:T(8,128)}, u32[]{:S(2)}) copy-start(f32[24,24,1,1,1]{1,0,4,3,2:T(8,128)} %constant.139) | copy-start | bytes 6916
  91.3 7.8 %copy-start.2 = (f32[24,6,3,9,129]{4,0,3,2,1:T(8,128)S(1)}, f32[24,6,3,9,129]{4,0,3,2,1:T(8,128)}, u32[]{:S(2)}) copy-start(f32[24,6,3,9,129]{4,0,3,2,1:T(8,128)} %reshape.550) | copy-start | bytes 6018628
  91.3 12.7 %slice-start = ((s8[5308416]{0:T(1024)(128)(4,1)}), s8[4194304]{0:T(1024)(128)(4,1)S(1)}, s32[]{:S(2)}) async-start(s8[5308416]{0:T(1024)(128)(4,1)} %bitcast.1302), calls=%async_computation | async-start | bytes 8388608
  142.6 9.8 %copy-start.9 = (f32[3,24,2,8,128]{4,3,2,1,0:T(8,128)S(1)}, f32[3,24,2,8,128]{4,3,2,1,0:T(8,128)}, u32[]{:S(2)}) copy-start(f32[3,24,2,8,128]{4,3,2,1,0:T(8,128)} %param.7) | copy-start | bytes 1769476
  327.4 20.4 %copy-start.10 = (f32[3,24,2,8,128]{4,0,3,2,1:T(4,128)S(1)}, f32[3,24,2,8,128]{4,0,3,2,1:T(4,128)}, u32[]{:S(2)}) copy-start(f32[3,24,2,8,128]{4,0,3,2,1:T(4,128)} %get-tuple-element.18) | copy-start | bytes 1769476
  328.1 10.6 %collective-permute-start.6 = (f32[3,24,1,8,128]{4,0,3,2,1:T(4,128)S(1)}, f32[3,24,1,8,128]{4,0,3,2,1:T(4,128)S(1)}, u32[]{:S(2)}, u32[]{:S(2)}) collective-permute-start(f32[3,24,1,8,128]{4,0,3,2,1:T(4,128)S(1)} %get-tuple-element.103), channel_id=1, source_target_pairs={{0,8},{8,16},{16,24},{24,32},{32,40},{40,48},{48,56},{56,64},{64,7... | collective-permute-start | bytes 884744 | tf_op jit(solution)/shard_map/ppermute | solution.py:27
  330.2 11.2 %collective-permute-start.7 = (f32[3,24,1,8,128]{4,0,3,2,1:T(4,128)S(1)}, f32[3,24,1,8,128]{4,0,3,2,1:T(4,128)S(1)}, u32[]{:S(2)}, u32[]{:S(2)}) collective-permute-start(f32[3,24,1,8,128]{4,0,3,2,1:T(4,128)S(1)} %get-tuple-element.104), channel_id=1, source_target_pairs={{8,0},{16,8},{24,16},{32,24},{40,32},{48,40},{56,48},{64,56},{72,6... | collective-permute-start | bytes 884744 | tf_op jit(solution)/shard_map/ppermute | solution.py:28
  341.5 7.9 %collective-permute-start.8 = (f32[3,24,4,1,128]{4,0,3,2,1:T(4,128)S(1)}, f32[3,24,4,1,128]{4,0,3,2,1:T(4,128)S(1)}, u32[]{:S(2)}, u32[]{:S(2)}) collective-permute-start(f32[3,24,4,1,128]{4,0,3,2,1:T(4,128)S(1)} %get-tuple-element.81), channel_id=1, source_target_pairs={{0,1},{1,2},{2,3},{3,4},{4,5},{5,6},{6,7},{8,9},{9,10},{10,11},{11... | collective-permute-start | bytes 442376 | tf_op jit(solution)/shard_map/ppermute | solution.py:27
  344.2 11.0 %collective-permute-start.9 = (f32[3,24,4,1,128]{4,0,3,2,1:T(4,128)S(1)}, f32[3,24,4,1,128]{4,0,3,2,1:T(4,128)S(1)}, u32[]{:S(2)}, u32[]{:S(2)}) collective-permute-start(f32[3,24,4,1,128]{4,0,3,2,1:T(4,128)S(1)} %get-tuple-element.82), channel_id=1, source_target_pairs={{1,0},{2,1},{3,2},{4,3},{5,4},{6,5},{7,6},{9,8},{10,9},{11,10},{12... | collective-permute-start | bytes 442376 | tf_op jit(solution)/shard_map/ppermute | solution.py:28
  359.4 7.3 %copy-start = (f32[3,24,4,10,130]{4,0,3,2,1:T(4,128)}, f32[3,24,4,10,130]{4,0,3,2,1:T(4,128)S(1)}, u32[]{:S(2)}) copy-start(f32[3,24,4,10,130]{4,0,3,2,1:T(4,128)S(1)} %select_maximum_fusion) | copy-start | bytes 4492804
  553.5 6.1 %collective-permute-start.10 = (f32[3,24,1,8,128]{4,1,3,2,0:T(8,128)S(1)}, f32[3,24,1,8,128]{4,1,3,2,0:T(8,128)S(1)}, u32[]{:S(2)}, u32[]{:S(2)}) collective-permute-start(f32[3,24,1,8,128]{4,1,3,2,0:T(8,128)S(1)} %slice.2277), channel_id=1, source_target_pairs={{8,0},{16,8},{24,16},{32,24},{40,32},{48,40},{56,48},{64,56},{72,6... | collective-permute-start | bytes 884744 | tf_op jit(solution)/shard_map/ppermute | solution.py:17
  559.6 7.7 %collective-permute-start.11 = (f32[3,24,3,1,128]{4,1,3,2,0:T(8,128)S(1)}, f32[3,24,3,1,128]{4,1,3,2,0:T(8,128)S(1)}, u32[]{:S(2)}, u32[]{:S(2)}) collective-permute-start(f32[3,24,3,1,128]{4,1,3,2,0:T(8,128)S(1)} %pad_maximum_fusion.8), channel_id=1, source_target_pairs={{1,0},{2,1},{3,2},{4,3},{5,4},{6,5},{7,6},{9,8},{10,9},{11,10},{12... | collective-permute-start | bytes 331784 | tf_op jit(solution)/shard_map/ppermute | solution.py:17
  573.3 5.2 copy-start.12
  578.5 7.9 %collective-permute-start.13 = (f32[2,2,8,128]{3,2,1,0:T(8,128)S(1)}, f32[2,2,8,128]{3,2,1,0:T(8,128)S(1)}, u32[]{:S(2)}, u32[]{:S(2)}) collective-permute-start(f32[2,2,8,128]{3,2,1,0:T(8,128)S(1)} %stack.455), channel_id=1, source_target_pairs={{8,0},{16,8},{24,16},{32,24},{40,32},{48,40},{56,48},{64,56},{72,6... | collective-permute-start | bytes 49160 | tf_op jit(solution)/shard_map/ppermute | solution.py:28
  584.4 6.6 %collective-permute-start.12 = (f32[2,2,8,128]{3,2,1,0:T(8,128)S(1)}, f32[2,2,8,128]{3,2,1,0:T(8,128)S(1)}, u32[]{:S(2)}, u32[]{:S(2)}) collective-permute-start(f32[2,2,8,128]{3,2,1,0:T(8,128)S(1)} %stack.455), channel_id=1, source_target_pairs={{0,8},{8,16},{16,24},{24,32},{32,40},{40,48},{48,56},{56,64},{64,7... | collective-permute-start | bytes 49160 | tf_op jit(solution)/shard_map/ppermute | solution.py:27
  591.0 5.9 collective-permute-start.14
  593.3 6.5 %collective-permute-start.15 = (f32[2,6,2,128]{3,2,1,0:T(2,128)S(1)}, f32[2,6,2,128]{3,2,1,0:T(2,128)S(1)}, u32[]{:S(2)}, u32[]{:S(2)}) collective-permute-start(f32[2,6,2,128]{3,2,1,0:T(2,128)S(1)} %get-tuple-element.117), channel_id=1, source_target_pairs={{1,0},{2,1},{3,2},{4,3},{5,4},{6,5},{7,6},{9,8},{10,9},{11,10},{12... | collective-permute-start | bytes 36872 | tf_op jit(solution)/shard_map/ppermute | solution.py:28
  (7 other events, 19.1 us)
